TPU v7x, 32 devices: a whole 2x2x4 slice. The times are simulated.
32 devices in a mesh: dp: 16 (over z, x, core), tensor: 2 (over y).
Axes of the slice: x: 2, y: 2, z: 4, core: 2. Of those that a mesh axis runs over, the one named last changes fastest.
Arguments:
- patches: bfloat16 [32768, 1280], P(('dp', 'tensor')), may hold values from -6 to 6
- positions: int32 [2, 32768], P(None, 'dp'), may hold values from 0 to 511, as said below
- ln1_gain: bfloat16 [1280], P(('dp', 'tensor')), may hold values from 0.099609375 to 1.8984375
- ln1_bias: bfloat16 [1280], P(('dp', 'tensor')), may hold values from -2 to 2
- w_qkv: bfloat16 [3, 1280, 1280], P(None, 'dp', 'tensor'), may hold values from -0.15625 to 0.15625
- b_qkv: bfloat16 [3, 1280], P(None, ('tensor', 'dp')), may hold values from -2 to 2
- w_out: bfloat16 [1280, 1280], P('tensor', 'dp'), may hold values from -1.25 to 1.25
- b_out: bfloat16 [1280], P(('dp', 'tensor')), may hold values from -2 to 2
- ln2_gain: bfloat16 [1280], P(('dp', 'tensor')), may hold values from 0.099609375 to 1.8984375
- ln2_bias: bfloat16 [1280], P(('dp', 'tensor')), may hold values from -2 to 2
- w_fc1: bfloat16 [1280, 5120], P('dp', 'tensor'), may hold values from -0.15625 to 0.15625
- b_fc1: bfloat16 [5120], P(('tensor', 'dp')), may hold values from -2 to 2
- w_fc2: bfloat16 [5120, 1280], P('tensor', 'dp'), may hold values from -0.125 to 0.125
- b_fc2: bfloat16 [1280], P(('dp', 'tensor')), may hold values from -2 to 2
- cotangent: bfloat16 [32768, 1280], P(('dp', 'tensor')), may hold values from -6 to 6
Outputs:
- result: bfloat16 [32768, 1280], P(('dp', 'tensor'))
- grad_patches: float32 [32768, 1280], P(('dp', 'tensor'))
- grad_ln1_gain: float32 [1280], P(('dp', 'tensor'))
- grad_ln1_bias: float32 [1280], P(('dp', 'tensor'))
- grad_w_qkv: float32 [3, 1280, 1280], P(None, 'dp', 'tensor')
- grad_b_qkv: float32 [3, 1280], P(None, ('tensor', 'dp'))
- grad_w_out: float32 [1280, 1280], P('tensor', 'dp')
- grad_b_out: float32 [1280], P(('dp', 'tensor'))
- grad_ln2_gain: float32 [1280], P(('dp', 'tensor'))
- grad_ln2_bias: float32 [1280], P(('dp', 'tensor'))
- grad_w_fc1: float32 [1280, 5120], P('dp', 'tensor')
- grad_b_fc1: float32 [5120], P(('tensor', 'dp'))
- grad_w_fc2: float32 [5120, 1280], P('tensor', 'dp')
- grad_b_fc2: float32 [1280], P(('dp', 'tensor'))
Inputs may be any that keep to these rules, and one draw needn't show every extreme that they name: Each image's 1024 tokens lie on a grid whose numbers of rows and columns are powers of two, two or more each, in blocks of 2 x 2 neighbouring patches; the first row of positions holds patch rows, the second patch columns.
All inputs are finite; a program needn't handle non-finite values.
Results may differ from a plain program's by a relative error of at most 0.024.
Values may be sent and summed in bfloat16 or wider, within the bound.
No kernel may reach another device: no remote copies, remote signals or barrier semaphores. Data moves between devices by JAX's collectives and lax.ppermute only.
A program may use at most 320 MiB of HBM per device.

v0:
```python
import jax
import jax.numpy as jnp
from jax import lax
from jax.sharding import PartitionSpec as P

HD = 80
PATCHES = 1024
norm_eps = 1e-06
gelu_slope = 1.702
rope_base = 10000.0


def rotary_tables(positions):
    freq_index = jnp.arange(HD // 4, dtype=jnp.float32)
    inverse = rope_base ** (-(freq_index * 4.0) / HD)
    row_angle = positions[0].astype(jnp.float32)[:, None] * inverse[None, :]
    col_angle = positions[1].astype(jnp.float32)[:, None] * inverse[None, :]
    angles = jnp.concatenate([row_angle, col_angle, row_angle, col_angle], axis=1)
    return (jnp.cos(angles), jnp.sin(angles))


def rotate(head_rows, cosine_table, sine_table):
    half_width = head_rows.shape[-1] // 2
    turned = jnp.concatenate([-head_rows[..., half_width:], head_rows[..., :half_width]], axis=-1)
    return head_rows * cosine_table[:, None, :] + turned * sine_table[:, None, :]


def rotate_back(grad_rows, cosine_table, sine_table):
    half_width = grad_rows.shape[-1] // 2
    with_sine = grad_rows * sine_table[:, None, :]
    turned = jnp.concatenate([with_sine[..., half_width:], -with_sine[..., :half_width]], axis=-1)
    return grad_rows * cosine_table[:, None, :] + turned


def norm_stats(rows_in):
    center = jnp.mean(rows_in, axis=-1, keepdims=True)
    shifted = rows_in - center
    variance = jnp.mean(shifted * shifted, axis=-1, keepdims=True)
    inv_root = lax.rsqrt(variance + norm_eps)
    return (shifted * inv_root, inv_root)


def norm_back(grad_norm, normal_rows, inv_root, norm_gain):
    scaled = grad_norm * norm_gain
    return inv_root * (
        scaled
        - jnp.mean(scaled, axis=-1, keepdims=True)
        - normal_rows * jnp.mean(scaled * normal_rows, axis=-1, keepdims=True)
    )


def attend(members):
    query_block, key_block, value_block = members
    scores = jnp.einsum(
        "qhd,khd->hqk", query_block, key_block, preferred_element_type=jnp.float32
    ) * HD ** (-0.5)
    row_top = jnp.max(scores, axis=-1, keepdims=True)
    exp_scores = jnp.exp(scores - row_top)
    row_total = jnp.sum(exp_scores, axis=-1, keepdims=True)
    weights_soft = (exp_scores / row_total).astype(jnp.bfloat16)
    mixed_heads = jnp.einsum(
        "hqk,khd->qhd", weights_soft, value_block, preferred_element_type=jnp.float32
    )
    return (mixed_heads, (row_top + jnp.log(row_total))[..., 0])


def attend_back(members):
    query_block, key_block, value_block, lse_block, grad_block = members
    scores = jnp.einsum(
        "qhd,khd->hqk", query_block, key_block, preferred_element_type=jnp.float32
    ) * HD ** (-0.5)
    weights_soft = jnp.exp(scores - lse_block[..., None])
    grad_weights = jnp.einsum(
        "qhd,khd->hqk", grad_block, value_block, preferred_element_type=jnp.float32
    )
    inner_sum = jnp.sum(weights_soft * grad_weights, axis=-1, keepdims=True)
    grad_scores = (weights_soft * (grad_weights - inner_sum)).astype(jnp.bfloat16)
    grad_values = jnp.einsum(
        "hqk,qhd->khd",
        weights_soft.astype(jnp.bfloat16),
        grad_block,
        preferred_element_type=jnp.float32,
    )
    grad_queries = jnp.einsum(
        "hqk,khd->qhd", grad_scores, key_block, preferred_element_type=jnp.float32
    ) * HD ** (-0.5)
    grad_keys = jnp.einsum(
        "hqk,qhd->khd", grad_scores, query_block, preferred_element_type=jnp.float32
    ) * HD ** (-0.5)
    return (grad_queries, grad_keys, grad_values)


def local(
    patches,
    positions,
    ln1_gain,
    ln1_bias,
    w_qkv,
    b_qkv,
    w_out,
    b_out,
    ln2_gain,
    ln2_bias,
    w_fc1,
    b_fc1,
    w_fc2,
    b_fc2,
    cotangent,
):
    group_rows = positions.shape[1]
    images_here = group_rows // PATCHES
    heads_here = w_qkv.shape[2] // HD
    vector_list = (
        lax.all_gather(ln1_gain, ("dp", "tensor"), axis=0, tiled=True),
        lax.all_gather(ln1_bias, ("dp", "tensor"), axis=0, tiled=True),
        lax.all_gather(b_out, ("dp", "tensor"), axis=0, tiled=True),
        lax.all_gather(ln2_gain, ("dp", "tensor"), axis=0, tiled=True),
        lax.all_gather(ln2_bias, ("dp", "tensor"), axis=0, tiled=True),
        lax.all_gather(b_fc2, ("dp", "tensor"), axis=0, tiled=True),
    )
    gain_one, shift_one, out_bias, gain_two, shift_two, fc2_bias = [
        item.astype(jnp.float32) for item in vector_list
    ]
    qkv_full, out_full, fc1_full, fc2_full, qkv_bias, fc1_bias = (
        lax.all_gather(w_qkv, "dp", axis=1, tiled=True),
        lax.all_gather(w_out, "dp", axis=1, tiled=True),
        lax.all_gather(w_fc1, "dp", axis=0, tiled=True),
        lax.all_gather(w_fc2, "dp", axis=1, tiled=True),
        lax.all_gather(b_qkv, "dp", axis=1, tiled=True),
        lax.all_gather(b_fc1, "dp", axis=0, tiled=True),
    )
    rows_in = patches.astype(jnp.float32)
    normal_one, root_one = norm_stats(rows_in)
    normed_one = (normal_one * gain_one + shift_one).astype(jnp.bfloat16)
    normed_all = lax.all_gather(normed_one, "tensor", axis=0, tiled=True)
    cosine_table, sine_table = rotary_tables(positions)
    projected = (
        jnp.einsum("ld,jde->jle", normed_all, qkv_full, preferred_element_type=jnp.float32)
        + qkv_bias.astype(jnp.float32)[:, None, :]
    )
    split_heads = projected.reshape(3, group_rows, heads_here, HD)
    queries = rotate(split_heads[0], cosine_table, sine_table).astype(jnp.bfloat16)
    keys_rot = rotate(split_heads[1], cosine_table, sine_table).astype(jnp.bfloat16)
    values_all = split_heads[2].astype(jnp.bfloat16)
    image_shape = (images_here, PATCHES, heads_here, HD)
    mixed_heads, log_totals = lax.map(
        attend,
        (
            queries.reshape(image_shape),
            keys_rot.reshape(image_shape),
            values_all.reshape(image_shape),
        ),
    )
    heads_mix = mixed_heads.reshape(group_rows, heads_here * HD).astype(jnp.bfloat16)
    rows_part = heads_mix
    attn_share = lax.psum_scatter(
        jnp.dot(rows_part, out_full, preferred_element_type=jnp.float32).astype(jnp.bfloat16),
        "tensor",
        scatter_dimension=0,
        tiled=True,
    ).astype(jnp.float32)
    hidden = rows_in + (attn_share + out_bias)
    normal_two, root_two = norm_stats(hidden)
    normed_two = (normal_two * gain_two + shift_two).astype(jnp.bfloat16)
    normed_two_all = lax.all_gather(normed_two, "tensor", axis=0, tiled=True)
    pre_act = jnp.dot(
        normed_two_all, fc1_full, preferred_element_type=jnp.float32
    ) + fc1_bias.astype(jnp.float32)
    gate_sig = jax.nn.sigmoid(gelu_slope * pre_act)
    activation = (pre_act * gate_sig).astype(jnp.bfloat16)
    rows_part = activation
    mlp_share = lax.psum_scatter(
        jnp.dot(rows_part, fc2_full, preferred_element_type=jnp.float32).astype(jnp.bfloat16),
        "tensor",
        scatter_dimension=0,
        tiled=True,
    ).astype(jnp.float32)
    result = (hidden + (mlp_share + fc2_bias)).astype(jnp.bfloat16)
    qkv_back, out_back, fc1_back, fc2_back = (
        lax.all_gather(w_qkv, "dp", axis=1, tiled=True),
        lax.all_gather(w_out, "dp", axis=1, tiled=True),
        lax.all_gather(w_fc1, "dp", axis=0, tiled=True),
        lax.all_gather(w_fc2, "dp", axis=1, tiled=True),
    )
    grad_out = cotangent.astype(jnp.float32)
    grad_fc2_bias = jnp.sum(grad_out, axis=0)
    grad_mlp_all = lax.all_gather(cotangent, "tensor", axis=0, tiled=True)
    grad_fc2_w = jnp.einsum(
        "lf,ld->fd", activation, grad_mlp_all, preferred_element_type=jnp.float32
    )
    grad_act = jnp.einsum("ld,fd->lf", grad_mlp_all, fc2_back, preferred_element_type=jnp.float32)
    gelu_grad = gate_sig + gelu_slope * pre_act * gate_sig * (1.0 - gate_sig)
    grad_pre = (grad_act * gelu_grad).astype(jnp.bfloat16)
    grad_fc1_bias = jnp.sum(grad_pre.astype(jnp.float32), axis=0)
    grad_fc1_w = jnp.einsum(
        "ld,lf->df", normed_two_all, grad_pre, preferred_element_type=jnp.float32
    )
    rows_part = grad_pre
    grad_norm_two = lax.psum_scatter(
        jnp.einsum("lf,df->ld", rows_part, fc1_back, preferred_element_type=jnp.float32).astype(
            jnp.bfloat16
        ),
        "tensor",
        scatter_dimension=0,
        tiled=True,
    ).astype(jnp.float32)
    grad_gain_two = jnp.sum(grad_norm_two * normal_two, axis=0)
    grad_shift_two = jnp.sum(grad_norm_two, axis=0)
    grad_hidden = grad_out + norm_back(grad_norm_two, normal_two, root_two, gain_two)
    grad_attn = grad_hidden.astype(jnp.bfloat16)
    grad_out_bias = jnp.sum(grad_attn.astype(jnp.float32), axis=0)
    grad_attn_all = lax.all_gather(grad_attn, "tensor", axis=0, tiled=True)
    grad_out_w = jnp.einsum(
        "le,ld->ed", heads_mix, grad_attn_all, preferred_element_type=jnp.float32
    )
    grad_heads = jnp.einsum(
        "ld,ed->le", grad_attn_all, out_back, preferred_element_type=jnp.float32
    ).astype(jnp.bfloat16)
    grad_queries, grad_keys, grad_values = lax.map(
        attend_back,
        (
            queries.reshape(image_shape),
            keys_rot.reshape(image_shape),
            values_all.reshape(image_shape),
            log_totals,
            grad_heads.reshape(image_shape),
        ),
    )
    flat_shape = (group_rows, heads_here, HD)
    grad_proj_q = rotate_back(grad_queries.reshape(flat_shape), cosine_table, sine_table).astype(
        jnp.bfloat16
    )
    grad_proj_k = rotate_back(grad_keys.reshape(flat_shape), cosine_table, sine_table).astype(
        jnp.bfloat16
    )
    grad_proj_v = grad_values.reshape(flat_shape).astype(jnp.bfloat16)
    grad_proj = jnp.stack([grad_proj_q, grad_proj_k, grad_proj_v], axis=0).reshape(
        3, group_rows, heads_here * HD
    )
    grad_qkv_bias = jnp.sum(grad_proj.astype(jnp.float32), axis=1)
    grad_qkv_w = jnp.einsum(
        "ld,jle->jde", normed_all, grad_proj, preferred_element_type=jnp.float32
    )
    rows_part = grad_proj
    grad_norm_one = lax.psum_scatter(
        jnp.einsum("jle,jde->ld", rows_part, qkv_back, preferred_element_type=jnp.float32).astype(
            jnp.bfloat16
        ),
        "tensor",
        scatter_dimension=0,
        tiled=True,
    ).astype(jnp.float32)
    grad_gain_one = jnp.sum(grad_norm_one * normal_one, axis=0)
    grad_shift_one = jnp.sum(grad_norm_one, axis=0)
    grad_patches = grad_hidden + norm_back(grad_norm_one, normal_one, root_one, gain_one)
    grad_qkv_s, grad_out_s, grad_fc1_s, grad_fc2_s, grad_qkv_bias_s, grad_fc1_bias_s = (
        lax.psum_scatter(
            grad_qkv_w.astype(jnp.bfloat16), "dp", scatter_dimension=1, tiled=True
        ).astype(jnp.float32),
        lax.psum_scatter(
            grad_out_w.astype(jnp.bfloat16), "dp", scatter_dimension=1, tiled=True
        ).astype(jnp.float32),
        lax.psum_scatter(
            grad_fc1_w.astype(jnp.bfloat16), "dp", scatter_dimension=0, tiled=True
        ).astype(jnp.float32),
        lax.psum_scatter(
            grad_fc2_w.astype(jnp.bfloat16), "dp", scatter_dimension=1, tiled=True
        ).astype(jnp.float32),
        lax.psum_scatter(
            grad_qkv_bias.astype(jnp.bfloat16), "dp", scatter_dimension=1, tiled=True
        ).astype(jnp.float32),
        lax.psum_scatter(
            grad_fc1_bias.astype(jnp.bfloat16), "dp", scatter_dimension=0, tiled=True
        ).astype(jnp.float32),
    )
    (
        grad_gain_one_s,
        grad_shift_one_s,
        grad_out_bias_s,
        grad_gain_two_s,
        grad_shift_two_s,
        grad_fc2_bias_s,
    ) = (
        lax.psum_scatter(grad_gain_one, ("dp", "tensor"), scatter_dimension=0, tiled=True),
        lax.psum_scatter(grad_shift_one, ("dp", "tensor"), scatter_dimension=0, tiled=True),
        lax.psum_scatter(grad_out_bias, ("dp", "tensor"), scatter_dimension=0, tiled=True),
        lax.psum_scatter(grad_gain_two, ("dp", "tensor"), scatter_dimension=0, tiled=True),
        lax.psum_scatter(grad_shift_two, ("dp", "tensor"), scatter_dimension=0, tiled=True),
        lax.psum_scatter(grad_fc2_bias, ("dp", "tensor"), scatter_dimension=0, tiled=True),
    )
    return (
        result,
        grad_patches,
        grad_gain_one_s,
        grad_shift_one_s,
        grad_qkv_s,
        grad_qkv_bias_s,
        grad_out_s,
        grad_out_bias_s,
        grad_gain_two_s,
        grad_shift_two_s,
        grad_fc1_s,
        grad_fc1_bias_s,
        grad_fc2_s,
        grad_fc2_bias_s,
    )


def solution(mesh):
    in_specs = (
        P(("dp", "tensor"), None),
        P(None, "dp"),
        P(("dp", "tensor")),
        P(("dp", "tensor")),
        P(None, "dp", "tensor"),
        P(None, ("tensor", "dp")),
        P("tensor", "dp"),
        P(("dp", "tensor")),
        P(("dp", "tensor")),
        P(("dp", "tensor")),
        P("dp", "tensor"),
        P(("tensor", "dp")),
        P("tensor", "dp"),
        P(("dp", "tensor")),
        P(("dp", "tensor"), None),
    )
    out_specs = (
        P(("dp", "tensor"), None),
        P(("dp", "tensor"), None),
        P(("dp", "tensor")),
        P(("dp", "tensor")),
        P(None, "dp", "tensor"),
        P(None, ("tensor", "dp")),
        P("tensor", "dp"),
        P(("dp", "tensor")),
        P(("dp", "tensor")),
        P(("dp", "tensor")),
        P("dp", "tensor"),
        P(("tensor", "dp")),
        P("tensor", "dp"),
        P(("dp", "tensor")),
    )
    return jax.shard_map(local, mesh=mesh, in_specs=in_specs, out_specs=out_specs, check_vma=False)
```

profile of v0, /device:TPU:0, one launch (start us, length us, event | category | flops | bytes accessed | tf_op | source)
XLA Modules:
  0.0 1690.3 jit_solution(3997134643809691741)
XLA Ops:
  13.8 42.6 %all-reduce.17 = (bf16[1280]{0:T(1024)(128)(2,1)}, bf16[1280]{0:T(1024)(128)(2,1)}, bf16[1280]{0:T(1024)(128)(2,1)}, bf16[1280]{0:T(1024)(128)(2,1)S(1)}, bf16[1...) all-reduce(bf16[1280]{0:T(1024)(128)(2,1)S(1)} %dynamic-update-slic, ...), channel_id=1, replica_groups=mesh['dp'=16,'tensor'=2] {'dp','tensor'}, use_global_device_ids=true, to_apply=%add.4 | all-reduce | flops 7680 | bytes 30720
  61.5 21.4 %all-gather = bf16[16,40,3]{1,2,0:T(4,128)(2,1)S(1)} all-gather(bf16[1,40,3]{1,2,0:T(4,128)(2,1)S(1)} %bitcast.215), channel_id=1, replica_groups=mesh['dp'=16,'tensor'=2] {'dp'}, dimensions={0}, use_global_device_ids=true | all-gather | bytes 4080 | tf_op jit(solution)/shard_map/all_gather | solution.py:129
  94.7 33.5 %all-gather.10.cloned.1.call-done = bf16[2048,1280]{1,0:T(8,128)(2,1)} async-done(((bf16[1024,1280]{1,0:T(8,128)(2,1)}), bf16[2048,1280]{1,0:T(8,128)(2,1)}) %all-gather.10.cloned.1.call-update) | async-done | bytes 5242896 | tf_op jit(solution)/shard_map/all_gather | solution.py:135
  128.2 56.4 %all-gather.12.cloned.1.call-done = bf16[3,1280,640]{2,1,0:T(8,128)(2,1)} async-done(((bf16[3,80,640]{2,1,0:T(8,128)(2,1)}), bf16[3,1280,640]{2,1,0:T(8,128)(2,1)}) %all-gather.12.cloned.1.call-update) | async-done | bytes 4915216 | tf_op jit(solution)/shard_map/all_gather | solution.py:125
  296.1 85.3 %while.28 = (s32[]{:T(128)}, bf16[2,1024,8,80]{1,3,2,0:T(8,128)(2,1)}, f32[2,8,1024]{2,1,0:T(8,128)S(1)}, bf16[2,1024,8,80]{1,3,2,0:T(8,128)(2,1)}, bf16[2,1024,...) while((s32[]{:T(128)}, bf16[2,1024,8,80]{1,3,2,0:T(8,128)(2,1)}, ...), condition=%wide.region_5.6_spmd.clone, body=%wide.region_2.5_spmd.sunk.clone | while | flops 2759843840 | bytes 117966952 | solution.py:146
  398.9 63.5 %reduce-scatter.9.cloned.1.call-done = bf16[1024,1280]{1,0:T(8,128)(2,1)} async-done(((bf16[2048,1280]{1,0:T(8,128)(2,1)}), bf16[1024,1280]{1,0:T(8,128)(2,1)}) %reduce-scatter.9.cloned.1.call-update) | async-done | bytes 2621456 | tf_op jit(solution)/shard_map/reduce_scatter | solution.py:156
  473.2 35.0 %all-reduce.5 = bf16[2560]{0:T(1024)(128)(2,1)S(1)} all-reduce(bf16[2560]{0:T(1024)(128)(2,1)S(1)} %dynamic-update-slice.5), channel_id=1, replica_groups=mesh['dp'=16,'tensor'=2] {'dp'}, use_global_device_ids=true, to_apply=%add.5 | all-reduce | flops 2560 | bytes 10240
  528.0 69.5 %all-gather.16.cloned.1.call-done = bf16[2048,1280]{1,0:T(8,128)(2,1)} async-done(((bf16[1024,1280]{1,0:T(8,128)(2,1)}), bf16[2048,1280]{1,0:T(8,128)(2,1)}) %all-gather.16.cloned.1.call-update) | async-done | bytes 5242896 | tf_op jit(solution)/shard_map/all_gather | solution.py:165
  597.4 25.9 %multiply_convert_fusion.2 = (bf16[2048,2560]{1,0:T(8,128)(2,1)}, f32[2048,2560]{1,0:T(8,128)}) fusion(f32[2560]{0:T(1024)S(1)} %convert_element_type.227, bf16[2048,1280]{1,0:T(8,128)(2,1)} %all-gather.16.cloned.1.call-done, bf16[1280,2560]{1,0:T(8,128)(2,1)} %all-gather.18.cloned.1.call-done), kind=kOutput, calls=%fused_computation.49 | convolution fusion | flops 13458472960 | bytes 43264000 | tf_op jit(solution)/shard_map/dot_general | solution.py:166
  623.3 44.2 %all-gather.22.cloned.1.call-done = bf16[2048,1280]{1,0:T(8,128)(2,1)} async-done(((bf16[1024,1280]{1,0:T(8,128)(2,1)}), bf16[2048,1280]{1,0:T(8,128)(2,1)}) %all-gather.22.cloned.1.call-update) | async-done | bytes 5242896 | tf_op jit(solution)/shard_map/all_gather | solution.py:187
  667.5 65.2 %all-gather.20.cloned.1.call-done = bf16[2560,1280]{0,1:T(8,128)(2,1)} async-done(((bf16[2560,80]{0,1:T(8,128)(2,1)}), bf16[2560,1280]{0,1:T(8,128)(2,1)}) %all-gather.20.cloned.1.call-update) | async-done | bytes 6553616 | tf_op jit(solution)/shard_map/all_gather | solution.py:128
  732.7 29.9 %fusion.87 = (bf16[2560]{0:T(1024)(128)(2,1)}, bf16[2048,2560]{1,0:T(8,128)(2,1)}) fusion(f32[2048,2560]{1,0:T(8,128)} %get-tuple-element.311, f32[2560]{0:T(1024)S(1)} %convert_element_type.227, bf16[2048,1280]{1,0:T(8,128)(2,1)} %all-gather.22.cloned.1.call-done, bf16[2560,1280]{0,1:T(8,128)(2,1)} %all-gather.20.cloned.1.call-done), kind=kOutput, calls=%fused_computation.157 | convolution fusion | flops 13484685312 | bytes 43269120 | tf_op jit(solution)/shard_map/ld,fd->lf/dot_general | solution.py:191
  802.3 44.3 %reduce-scatter.13.cloned.1.call-done = bf16[1024,1280]{1,0:T(8,128)(2,1)} async-done(((bf16[2048,1280]{1,0:T(8,128)(2,1)}), bf16[1024,1280]{1,0:T(8,128)(2,1)}) %reduce-scatter.13.cloned.1.call-update) | async-done | bytes 2621456 | tf_op jit(solution)/shard_map/reduce_scatter | solution.py:199
  852.4 62.2 %reduce-scatter.11.cloned.1.call-done = bf16[1024,1280]{1,0:T(8,128)(2,1)} async-done(((bf16[2048,1280]{1,0:T(8,128)(2,1)}), bf16[1024,1280]{1,0:T(8,128)(2,1)}) %reduce-scatter.11.cloned.1.call-update) | async-done | bytes 2621456 | tf_op jit(solution)/shard_map/reduce_scatter | solution.py:172
  1015.8 213.5 %while.29 = (s32[]{:T(128)}, f32[2,1024,8,80]{1,3,2,0:T(8,128)}, f32[2,1024,8,80]{1,3,2,0:T(8,128)}, bf16[2,1024,8,80]{1,3,2,0:T(8,128)(2,1)}, bf16[2,1024,8,80]...) while((s32[]{:T(128)}, f32[2,1024,8,80]{1,3,2,0:T(8,128)}, ...), condition=%wide.region_15.16_spmd.clone, body=%wide.region_13.15_spmd.sunk.clone | while | flops 6812852224 | bytes 268932192 | solution.py:219
  1046.6 23.4 %multiply_reduce_fusion.8 = (f32[8,1024]{1,0:T(8,128)S(1)}, f32[8,1024,1024]{1,2,0:T(8,128)}) fusion(f32[8,1024,1024]{1,2,0:T(8,128)} %fusion.142, f32[8,1024]{1,0:T(8,128)S(1)} %dynamic-slice_bitcast_fusion.3, bf16[2,1024,8,80]{1,3,2,0:T(8,128)(2,1)} %get-tuple-element.498, s32[]{:T(128)S(6)} %copy.173, ...), kind=kOutput, calls=%fused_computation.18.clone.1.clone | convolution fusion | flops 1375723520 | bytes 69796864 | tf_op jit(solution)/shard_map/while/body/eval_jaxpr/qhd,khd->hqk/dot_general | solution.py:73
  1070.0 29.1 %multiply_convert_fusion.5 = bf16[8,1024,1024]{1,2,0:T(8,128)(2,1)} fusion(f32[8,1024,1024]{1,2,0:T(8,128)} %get-tuple-element.442, f32[8,1024,1024]{1,2,0:T(8,128)} %fusion.142, f32[8,1024]{1,0:T(8,128)S(1)} %get-tuple-element.443, f32[8,1024]{1,0:T(8,128)S(1)} %dynamic-slice_bitcast_fusion.3), kind=kLoop, calls=%fused_computation.17.clone.1.clone | loop fusion | flops 41943040 | bytes 83951616 | tf_op jit(solution)/shard_map/while/body/eval_jaxpr/convert_element_type | solution.py:77
  1154.4 23.4 %multiply_reduce_fusion.8 = (f32[8,1024]{1,0:T(8,128)S(1)}, f32[8,1024,1024]{1,2,0:T(8,128)}) fusion(f32[8,1024,1024]{1,2,0:T(8,128)} %fusion.142, f32[8,1024]{1,0:T(8,128)S(1)} %dynamic-slice_bitcast_fusion.3, bf16[2,1024,8,80]{1,3,2,0:T(8,128)(2,1)} %get-tuple-element.498, s32[]{:T(128)S(6)} %copy.173, ...), kind=kOutput, calls=%fused_computation.18.clone.1.clone | convolution fusion | flops 1375723520 | bytes 69796864 | tf_op jit(solution)/shard_map/while/body/eval_jaxpr/qhd,khd->hqk/dot_general | solution.py:73
  1177.8 28.2 %multiply_convert_fusion.5 = bf16[8,1024,1024]{1,2,0:T(8,128)(2,1)} fusion(f32[8,1024,1024]{1,2,0:T(8,128)} %get-tuple-element.442, f32[8,1024,1024]{1,2,0:T(8,128)} %fusion.142, f32[8,1024]{1,0:T(8,128)S(1)} %get-tuple-element.443, f32[8,1024]{1,0:T(8,128)S(1)} %dynamic-slice_bitcast_fusion.3), kind=kLoop, calls=%fused_computation.17.clone.1.clone | loop fusion | flops 41943040 | bytes 83951616 | tf_op jit(solution)/shard_map/while/body/eval_jaxpr/convert_element_type | solution.py:77
  1393.3 62.2 %all-reduce.18 = (bf16[3,640]{1,0:T(4,128)(2,1)S(1)}, bf16[2560]{0:T(1024)(128)(2,1)S(1)}) all-reduce(bf16[3,640]{1,0:T(4,128)(2,1)S(1)} %fusion.83, bf16[2560]{0:T(1024)(128)(2,1)S(1)} %copy-done.37), channel_id=9, replica_groups=mesh['dp'=16,'tensor'=2] {'dp'}, use_global_device_ids=true, to_apply=%region_25.26.clone | all-reduce | flops 4480 | bytes 17920
  1456.8 44.6 %all-reduce.21.cloned.1.call-done = bf16[3,1280,640]{2,0,1:T(4,128)(2,1)} async-done(((bf16[3,1280,640]{2,0,1:T(4,128)(2,1)}), bf16[3,1280,640]{2,0,1:T(4,128)(2,1)}) %all-reduce.21.cloned.1.call-update) | async-done | bytes 4915216
  1503.3 59.9 %reduce-scatter.17.cloned.1.call-done = bf16[640,80]{0,1:T(8,128)(2,1)} async-done(((bf16[640,1280]{0,1:T(8,128)(2,1)}), bf16[640,80]{0,1:T(8,128)(2,1)}) %reduce-scatter.17.cloned.1.call-update) | async-done | bytes 102416 | tf_op jit(solution)/shard_map/reduce_scatter | solution.py:260
  1564.7 65.4 %reduce-scatter.15.cloned.1.call-done = bf16[1024,1280]{1,0:T(8,128)(2,1)} async-done(((bf16[2048,1280]{1,0:T(8,128)(2,1)}), bf16[1024,1280]{1,0:T(8,128)(2,1)}) %reduce-scatter.15.cloned.1.call-update) | async-done | bytes 2621456 | tf_op jit(solution)/shard_map/reduce_scatter | solution.py:245
  1634.2 40.0 %all-reduce.16 = (f32[1280]{0:T(1024)S(1)}, f32[1280]{0:T(1024)S(1)}, f32[1280]{0:T(1024)S(1)}, f32[1280]{0:T(1024)S(1)}, f32[1280]{0:T(1024)S(1)}, /*index=5*/f32[1280]{0:T(1024)S(1)}) all-reduce(f32[1280]{0:T(1024)S(1)} %get-tuple-element.219, ...), channel_id=6, replica_groups=mesh['dp'=16,'tensor'=2] {'dp','tensor'}, use_global_device_ids=true, to_apply=%region_20.21.clone | all-reduce | flops 7680 | bytes 61440
  (282 shorter events, 702.0 us)
Async XLA Ops:
  7.3 120.9 %all-gather.10.cloned.1.call-start = ((), (), s32[]{:S(2)}) async-start(), calls=%async_computation.7 | async-start | bytes 7864320 | tf_op jit(solution)/shard_map/all_gather | solution.py:135
  59.5 125.0 %all-gather.12.cloned.1.call-start = ((), (), s32[]{:S(2)}) async-start(), calls=%async_computation.8 | async-start | bytes 5222400 | tf_op jit(solution)/shard_map/all_gather | solution.py:125
  60.3 329.0 %all-gather.14.cloned.1.call-start = ((), (), s32[]{:S(2)}) async-start(), calls=%async_computation.9 | async-start | bytes 1740800 | tf_op jit(solution)/shard_map/all_gather | solution.py:126
  61.0 401.5 %reduce-scatter.9.cloned.1.call-start = ((), (), s32[]{:S(2)}) async-start(), calls=%async_computation.10 | async-start | bytes 7864320 | tf_op jit(solution)/shard_map/reduce_scatter | solution.py:156
  398.2 129.7 %all-gather.18.cloned.1.call-start = ((), (), s32[]{:S(2)}) async-start(), calls=%async_computation.12 | async-start | bytes 6963200 | tf_op jit(solution)/shard_map/all_gather | solution.py:127
  398.8 198.6 %all-gather.16.cloned.1.call-start = ((), (), s32[]{:S(2)}) async-start(), calls=%async_computation.11 | async-start | bytes 7864320 | tf_op jit(solution)/shard_map/all_gather | solution.py:165
  470.1 197.5 %all-gather.22.cloned.1.call-start = ((), (), s32[]{:S(2)}) async-start(), calls=%async_computation.15 | async-start | bytes 7864320 | tf_op jit(solution)/shard_map/all_gather | solution.py:187
  470.8 261.9 %all-gather.20.cloned.1.call-start = ((), (), s32[]{:S(2)}) async-start(), calls=%async_computation.13 | async-start | bytes 6963200 | tf_op jit(solution)/shard_map/all_gather | solution.py:128
  471.6 375.1 %reduce-scatter.13.cloned.1.call-start = ((), (), s32[]{:S(2)}) async-start(), calls=%async_computation.16 | async-start | bytes 7864320 | tf_op jit(solution)/shard_map/reduce_scatter | solution.py:199
  782.0 132.6 %reduce-scatter.11.cloned.1.call-start = ((), (), s32[]{:S(2)}) async-start(), calls=%async_computation.14 | async-start | bytes 7864320 | tf_op jit(solution)/shard_map/reduce_scatter | solution.py:172
  801.7 191.0 %all-gather.24.cloned.1.call-start = ((), (), s32[]{:S(2)}) async-start(), calls=%async_computation.17 | async-start | bytes 7864320 | tf_op jit(solution)/shard_map/all_gather | solution.py:212
  924.0 460.3 %reduce-scatter.21.cloned.1.call-start = ((), (), s32[]{:S(2)}) async-start(), calls=%async_computation.21 | async-start | bytes 6963200 | tf_op jit(solution)/shard_map/reduce_scatter | solution.py:266
  944.4 441.9 %reduce-scatter.19.cloned.1.call-start = ((), (), s32[]{:S(2)}) async-start(), calls=%async_computation.20 | async-start | bytes 6963200 | tf_op jit(solution)/shard_map/reduce_scatter | solution.py:263
  977.3 524.1 %all-reduce.21.cloned.1.call-start = ((), (), s32[]{:S(2)}) async-start(), calls=%async_computation.22 | async-start | bytes 13107200
  1357.2 205.9 %reduce-scatter.17.cloned.1.call-start = ((), (), s32[]{:S(2)}) async-start(), calls=%async_computation.19 | async-start | bytes 1740800 | tf_op jit(solution)/shard_map/reduce_scatter | solution.py:260
  1366.1 264.0 %reduce-scatter.15.cloned.1.call-start = ((), (), s32[]{:S(2)}) async-start(), calls=%async_computation.18 | async-start | bytes 7864320 | tf_op jit(solution)/shard_map/reduce_scatter | solution.py:245
  1388.2 241.8 %copy-start.3 = (bf16[1024,1280]{1,0:T(8,128)(2,1)S(1)}, bf16[1024,1280]{1,0:T(8,128)(2,1)}, u32[]{:S(2)}) copy-start(bf16[1024,1280]{1,0:T(8,128)(2,1)} %param.19) | copy-start | bytes 7864324
  1388.2 241.8 %copy-start.20 = (f32[1280]{0:T(1024)S(1)}, f32[1280]{0:T(1024)}, u32[]{:S(2)}) copy-start(f32[1280]{0:T(1024)} %copy-done.19) | copy-start | bytes 15364
  1388.2 241.8 %copy-start.26 = (f32[1024]{0:T(1024)S(1)}, f32[1024]{0:T(1024)}, u32[]{:S(2)}) copy-start(f32[1024]{0:T(1024)} %copy-done.25) | copy-start | bytes 12292
  1388.3 241.8 %copy-start.32 = (f32[1024]{0:T(1024)S(1)}, f32[1024]{0:T(1024)}, u32[]{:S(2)}) copy-start(f32[1024]{0:T(1024)} %copy-done.31) | copy-start | bytes 12292
  1393.2 241.0 %copy-start.33 = (f32[1280]{0:T(1024)S(1)}, f32[1280]{0:T(1024)}, u32[]{:S(2)}) copy-start(f32[1280]{0:T(1024)} %get-tuple-element.271) | copy-start | bytes 15364
  1393.2 241.0 %copy-start.34 = (f32[1280]{0:T(1024)S(1)}, f32[1280]{0:T(1024)}, u32[]{:S(2)}) copy-start(f32[1280]{0:T(1024)} %get-tuple-element.293) | copy-start | bytes 15364
  1393.2 241.0 %copy-start.35 = (f32[1280]{0:T(1024)S(1)}, f32[1280]{0:T(1024)}, u32[]{:S(2)}) copy-start(f32[1280]{0:T(1024)} %get-tuple-element.217) | copy-start | bytes 15364
  1393.2 241.0 %copy-start.36 = (f32[1280]{0:T(1024)S(1)}, f32[1280]{0:T(1024)}, u32[]{:S(2)}) copy-start(f32[1280]{0:T(1024)} %get-tuple-element.223) | copy-start | bytes 15364
  (47 other events, 957.7 us)
Sparse Core Ops, SparseCore 0:
  59.6 68.4 all-gather.9
  130.4 54.1 all-gather.11
  186.7 38.4 all-gather.13
  398.3 64.1 reduce-scatter.8
  464.6 63.2 all-gather.17
  529.9 67.4 all-gather.15
  599.0 68.5 all-gather.21
  669.8 62.8 all-gather.19
  782.1 64.4 reduce-scatter.12
  848.8 65.7 reduce-scatter.10
  924.1 68.5 all-gather.23
  996.5 86.7 reduce-scatter.20
  1087.3 85.7 reduce-scatter.18
  1357.3 143.9 all-reduce.20
  1504.9 58.1 reduce-scatter.16
  1565.3 64.7 reduce-scatter.14
where the time goes:
time: 1700 us; the launch traced here: 1690 us
  waiting for transfers between devices  647 us (38%)
  matrix products  424 us (25%)
  other arithmetic  203 us (12%)
  blocking collectives  201 us (12%)
  local copies, waits for them, and re-layouts  195 us (11%)
  between operations  17.6 us (1%)
    unnamed x4, blocking collectives  180 us
    all_gather x1, waiting for transfers between devices, local(): normed_two_all = lax.all_gather(normed_two, 'tensor', axis=0, tiled=True)  69.5 us
    reduce_scatter x1, waiting for transfers between devices, local(): lax.psum_scatter(jnp.einsum('jle,jde->ld', rows_part, qkv_back, preferred...  65.4 us
    all_gather x1, waiting for transfers between devices, local(): lax.all_gather(w_fc2, 'dp', axis=1, tiled=True)  65.2 us
    reduce_scatter x1, waiting for transfers between devices, local(): lax.psum_scatter(jnp.dot(rows_part, out_full, preferred_element_type=jnp....  63.5 us
    reduce_scatter x1, waiting for transfers between devices, local(): lax.psum_scatter(jnp.dot(rows_part, fc2_full, preferred_element_type=jnp....  62.2 us
    reduce_scatter x1, waiting for transfers between devices, local(): lax.psum_scatter(grad_out_w.astype(jnp.bfloat16), 'dp', scatter_dimension...  59.9 us
    convert_element_type x2, other arithmetic, attend_back(): (weights_soft * (grad_weights - inner_sum)).astype(jnp.bfloat16)  57.3 us
  transfers between devices with their start and end apart: 16, of which 13 were waited for; matrix products, arithmetic and copies ran while one was open for 43% of the time, Pallas kernels for 0%

commit v1 on v0

--- a/solution.py
+++ b/solution.py
@@ -8,6 +8,28 @@
 norm_eps = 1e-06
 gelu_slope = 1.702
 rope_base = 10000.0
+
+
+def in_order(blocks, dim):
+    dims = list(blocks.shape[1:])
+    dims[dim] *= blocks.shape[0]
+    return jnp.moveaxis(blocks, 0, dim).reshape(dims)
+
+
+def gather_around(shard, axis, dim):
+    peers = lax.axis_size(axis)
+    pairs = [(i, (i + 1) % peers) for i in range(peers)]
+    back = [(b, a) for a, b in pairs]
+    lower, upper = ([], [])
+    for step in range(peers - 1):
+        if step % 2 == 0:
+            lower.append(lax.ppermute(lower[-1] if lower else shard, axis, pairs))
+        else:
+            upper.append(lax.ppermute(upper[-1] if upper else shard, axis, back))
+    tiles = jnp.stack([*lower[::-1], shard, *upper])
+    shift = lax.axis_index(axis) - len(lower)
+    tiles = tiles[(jnp.arange(peers) - shift) % peers]
+    return in_order(tiles, dim)
 
 
 def rotary_tables(positions):
@@ -125,7 +147,7 @@
         lax.all_gather(w_qkv, "dp", axis=1, tiled=True),
         lax.all_gather(w_out, "dp", axis=1, tiled=True),
         lax.all_gather(w_fc1, "dp", axis=0, tiled=True),
-        lax.all_gather(w_fc2, "dp", axis=1, tiled=True),
+        gather_around(w_fc2, "dp", 1),
         lax.all_gather(b_qkv, "dp", axis=1, tiled=True),
         lax.all_gather(b_fc1, "dp", axis=0, tiled=True),
     )

time: 1700 us -> 1730 us (1.018)
  starting transfers between devices: 0.64 us -> 29.2 us
  local copies, waits for them, and re-layouts: 195 us -> 222 us
  waiting for transfers between devices: 647 us -> 625 us
    ppermute x0 -> x15, waiting for transfers between devices: none -> 65.9 us  [the longest x8 57.6 us: gather_around(): lower.append(lax.ppermute(lower[-1] if lower else shard, axis, pairs))]
    all_gather x1, waiting for transfers between devices: 69.5 us -> 18.6 us  [local(): normed_two_all = lax.all_gather(normed_two, 'tensor', axis=0, tiled=True)]
    ppermute x0 -> x15, starting transfers between devices: none -> 27.6 us  [the longest x7 27.5 us: gather_around(): upper.append(lax.ppermute(upper[-1] if upper else shard, axis, back))]
    all_gather x1, waiting for transfers between devices: 19.8 us -> 0.01 us  [local(): lax.all_gather(w_fc1, 'dp', axis=0, tiled=True)]
    unnamed x130 -> x153, local copies, waits for them, and re-layouts: 15.5 us -> 34.1 us
    reduce_scatter x1, waiting for transfers between devices: 44.3 us -> 25.9 us  [local(): lax.psum_scatter(jnp.einsum('lf,df->ld', rows_part, fc1_back, preferred_e...]
  transfers between devices with their start and end apart: 16 -> 31, of which waited for: 13 -> 22; matrix products, arithmetic and copies ran while one was open for 43% -> 47% of each run, Pallas kernels for 0% -> 0%
where the time goes in v1:
time: 1730 us; the launch traced here: 1720 us
  waiting for transfers between devices  625 us (36%)
  matrix products  424 us (25%)
  local copies, waits for them, and re-layouts  222 us (13%)
  other arithmetic  203 us (12%)
  blocking collectives  201 us (12%)
  starting transfers between devices  29.2 us (2%)
  between operations  17.6 us (1%)
    unnamed x4, blocking collectives  179 us
    reduce_scatter x1, waiting for transfers between devices, local(): lax.psum_scatter(jnp.einsum('jle,jde->ld', rows_part, qkv_back, preferred...  65.4 us
    all_gather x1, waiting for transfers between devices, local(): lax.all_gather(w_fc2, 'dp', axis=1, tiled=True)  65.2 us
    reduce_scatter x1, waiting for transfers between devices, local(): lax.psum_scatter(jnp.dot(rows_part, out_full, preferred_element_type=jnp....  63.5 us
    reduce_scatter x1, waiting for transfers between devices, local(): lax.psum_scatter(jnp.dot(rows_part, fc2_full, preferred_element_type=jnp....  62.2 us
    reduce_scatter x1, waiting for transfers between devices, local(): lax.psum_scatter(grad_out_w.astype(jnp.bfloat16), 'dp', scatter_dimension...  59.9 us
    ppermute x8, waiting for transfers between devices, gather_around(): lower.append(lax.ppermute(lower[-1] if lower else shard, axis, pairs))  57.6 us
    convert_element_type x2, other arithmetic, attend_back(): (weights_soft * (grad_weights - inner_sum)).astype(jnp.bfloat16)  57.4 us
  transfers between devices with their start and end apart: 31, of which 22 were waited for; matrix products, arithmetic and copies ran while one was open for 47% of the time, Pallas kernels for 0%

profile of v1, /device:TPU:0, one launch (start us, length us, event | category | flops | bytes accessed | tf_op | source)
XLA Modules:
  0.0 1722.1 jit_solution(1228601075170064269)
XLA Ops:
  13.8 42.6 %all-reduce.17 = (bf16[1280]{0:T(1024)(128)(2,1)}, bf16[1280]{0:T(1024)(128)(2,1)}, bf16[1280]{0:T(1024)(128)(2,1)}, bf16[1280]{0:T(1024)(128)(2,1)S(1)}, bf16[1...) all-reduce(bf16[1280]{0:T(1024)(128)(2,1)S(1)} %dynamic-update-slic, ...), channel_id=1, replica_groups=mesh['dp'=16,'tensor'=2] {'dp','tensor'}, use_global_device_ids=true, to_apply=%add.4 | all-reduce | flops 7680 | bytes 30720
  61.5 21.4 %all-gather = bf16[16,40,3]{1,2,0:T(4,128)(2,1)S(1)} all-gather(bf16[1,40,3]{1,2,0:T(4,128)(2,1)S(1)} %bitcast.253), channel_id=1, replica_groups=mesh['dp'=16,'tensor'=2] {'dp'}, dimensions={0}, use_global_device_ids=true | all-gather | bytes 4080 | tf_op jit(solution)/shard_map/all_gather | solution.py:151
  94.7 33.5 %all-gather.10.cloned.1.call-done = bf16[2048,1280]{1,0:T(8,128)(2,1)} async-done(((bf16[1024,1280]{1,0:T(8,128)(2,1)}), bf16[2048,1280]{1,0:T(8,128)(2,1)}) %all-gather.10.cloned.1.call-update) | async-done | bytes 5242896 | tf_op jit(solution)/shard_map/all_gather | solution.py:157
  128.2 56.4 %all-gather.12.cloned.1.call-done = bf16[3,1280,640]{2,1,0:T(8,128)(2,1)} async-done(((bf16[3,80,640]{2,1,0:T(8,128)(2,1)}), bf16[3,1280,640]{2,1,0:T(8,128)(2,1)}) %all-gather.12.cloned.1.call-update) | async-done | bytes 4915216 | tf_op jit(solution)/shard_map/all_gather | solution.py:147
  296.2 85.6 %while.28 = (s32[]{:T(128)}, bf16[2,1024,8,80]{1,3,2,0:T(8,128)(2,1)}, f32[2,8,1024]{2,1,0:T(8,128)S(1)}, bf16[2,1024,8,80]{1,3,2,0:T(8,128)(2,1)}, bf16[2,1024,...) while((s32[]{:T(128)}, bf16[2,1024,8,80]{1,3,2,0:T(8,128)(2,1)}, ...), condition=%wide.region_5.6_spmd.clone, body=%wide.region_2.5_spmd.sunk.clone | while | flops 2759843840 | bytes 117966952 | solution.py:168
  399.2 63.5 %reduce-scatter.9.cloned.1.call-done = bf16[1024,1280]{1,0:T(8,128)(2,1)} async-done(((bf16[2048,1280]{1,0:T(8,128)(2,1)}), bf16[1024,1280]{1,0:T(8,128)(2,1)}) %reduce-scatter.9.cloned.1.call-update) | async-done | bytes 2621456 | tf_op jit(solution)/shard_map/reduce_scatter | solution.py:178
  566.9 34.4 %all-reduce.5 = bf16[2560]{0:T(1024)(128)(2,1)S(1)} all-reduce(bf16[2560]{0:T(1024)(128)(2,1)S(1)} %dynamic-update-slice.5), channel_id=1, replica_groups=mesh['dp'=16,'tensor'=2] {'dp'}, use_global_device_ids=true, to_apply=%add.5 | all-reduce | flops 2560 | bytes 10240
  629.0 25.6 %multiply_convert_fusion.2 = (bf16[2048,2560]{1,0:T(8,128)(2,1)}, f32[2048,2560]{1,0:T(8,128)}) fusion(f32[2560]{0:T(1024)S(1)} %convert_element_type.227, bf16[2048,1280]{1,0:T(8,128)(2,1)} %all-gather.16.cloned.1.call-done, bf16[1280,2560]{1,0:T(8,128)(2,1)} %all-gather.18.cloned.1.call-done), kind=kOutput, calls=%fused_computation.50 | convolution fusion | flops 13458472960 | bytes 43264000 | tf_op jit(solution)/shard_map/dot_general | solution.py:188
  654.5 44.5 %all-gather.20.cloned.1.call-done = bf16[2048,1280]{1,0:T(8,128)(2,1)} async-done(((bf16[1024,1280]{1,0:T(8,128)(2,1)}), bf16[2048,1280]{1,0:T(8,128)(2,1)}) %all-gather.20.cloned.1.call-update) | async-done | bytes 5242896 | tf_op jit(solution)/shard_map/all_gather | solution.py:209
  699.1 65.2 %all-gather.22.cloned.1.call-done = bf16[2560,1280]{0,1:T(8,128)(2,1)} async-done(((bf16[2560,80]{0,1:T(8,128)(2,1)}), bf16[2560,1280]{0,1:T(8,128)(2,1)}) %all-gather.22.cloned.1.call-update) | async-done | bytes 6553616 | tf_op jit(solution)/shard_map/all_gather | solution.py:205
  764.2 29.9 %fusion.89 = (bf16[2560]{0:T(1024)(128)(2,1)}, bf16[2048,2560]{1,0:T(8,128)(2,1)}) fusion(f32[2048,2560]{1,0:T(8,128)} %get-tuple-element.311, f32[2560]{0:T(1024)S(1)} %convert_element_type.227, bf16[2048,1280]{1,0:T(8,128)(2,1)} %all-gather.20.cloned.1.call-done, bf16[2560,1280]{0,1:T(8,128)(2,1)} %all-gather.22.cloned.1.call-done), kind=kOutput, calls=%fused_computation.181 | convolution fusion | flops 13484685312 | bytes 43269120 | tf_op jit(solution)/shard_map/ld,fd->lf/dot_general | solution.py:213
  852.2 25.9 %reduce-scatter.13.cloned.1.call-done = bf16[1024,1280]{1,0:T(8,128)(2,1)} async-done(((bf16[2048,1280]{1,0:T(8,128)(2,1)}), bf16[1024,1280]{1,0:T(8,128)(2,1)}) %reduce-scatter.13.cloned.1.call-update) | async-done | bytes 2621456 | tf_op jit(solution)/shard_map/reduce_scatter | solution.py:221
  883.9 62.2 %reduce-scatter.11.cloned.1.call-done = bf16[1024,1280]{1,0:T(8,128)(2,1)} async-done(((bf16[2048,1280]{1,0:T(8,128)(2,1)}), bf16[1024,1280]{1,0:T(8,128)(2,1)}) %reduce-scatter.11.cloned.1.call-update) | async-done | bytes 2621456 | tf_op jit(solution)/shard_map/reduce_scatter | solution.py:194
  956.0 20.0 %convolution_convert_fusion = bf16[2560,1280]{0,1:T(8,128)(2,1)} fusion(bf16[2048,2560]{1,0:T(8,128)(2,1)} %get-tuple-element.310, bf16[2048,1280]{1,0:T(8,128)(2,1)} %all-gather.20.cloned.1.call-done), kind=kOutput, calls=%fused_computation.53 | convolution fusion | flops 13425049600 | bytes 22282240 | tf_op jit(solution)/shard_map/lf,ld->fd/dot_general | solution.py:210
  1047.3 213.6 %while.29 = (s32[]{:T(128)}, f32[2,1024,8,80]{1,3,2,0:T(8,128)}, f32[2,1024,8,80]{1,3,2,0:T(8,128)}, bf16[2,1024,8,80]{1,3,2,0:T(8,128)(2,1)}, bf16[2,1024,8,80]...) while((s32[]{:T(128)}, f32[2,1024,8,80]{1,3,2,0:T(8,128)}, ...), condition=%wide.region_15.16_spmd.clone, body=%wide.region_13.15_spmd.sunk.clone | while | flops 6812852224 | bytes 268932192 | solution.py:241
  1078.1 23.4 %multiply_reduce_fusion.8 = (f32[8,1024]{1,0:T(8,128)S(1)}, f32[8,1024,1024]{1,2,0:T(8,128)}) fusion(f32[8,1024,1024]{1,2,0:T(8,128)} %fusion.144, f32[8,1024]{1,0:T(8,128)S(1)} %dynamic-slice_bitcast_fusion.3, bf16[2,1024,8,80]{1,3,2,0:T(8,128)(2,1)} %get-tuple-element.498, s32[]{:T(128)S(6)} %copy.188, ...), kind=kOutput, calls=%fused_computation.19.clone.1.clone | convolution fusion | flops 1375723520 | bytes 69796864 | tf_op jit(solution)/shard_map/while/body/eval_jaxpr/qhd,khd->hqk/dot_general | solution.py:95
  1101.5 29.1 %multiply_convert_fusion.5 = bf16[8,1024,1024]{1,2,0:T(8,128)(2,1)} fusion(f32[8,1024,1024]{1,2,0:T(8,128)} %get-tuple-element.442, f32[8,1024,1024]{1,2,0:T(8,128)} %fusion.144, f32[8,1024]{1,0:T(8,128)S(1)} %get-tuple-element.443, f32[8,1024]{1,0:T(8,128)S(1)} %dynamic-slice_bitcast_fusion.3), kind=kLoop, calls=%fused_computation.18.clone.1.clone | loop fusion | flops 41943040 | bytes 83951616 | tf_op jit(solution)/shard_map/while/body/eval_jaxpr/convert_element_type | solution.py:99
  1186.0 23.4 %multiply_reduce_fusion.8 = (f32[8,1024]{1,0:T(8,128)S(1)}, f32[8,1024,1024]{1,2,0:T(8,128)}) fusion(f32[8,1024,1024]{1,2,0:T(8,128)} %fusion.144, f32[8,1024]{1,0:T(8,128)S(1)} %dynamic-slice_bitcast_fusion.3, bf16[2,1024,8,80]{1,3,2,0:T(8,128)(2,1)} %get-tuple-element.498, s32[]{:T(128)S(6)} %copy.188, ...), kind=kOutput, calls=%fused_computation.19.clone.1.clone | convolution fusion | flops 1375723520 | bytes 69796864 | tf_op jit(solution)/shard_map/while/body/eval_jaxpr/qhd,khd->hqk/dot_general | solution.py:95
  1209.3 28.3 %multiply_convert_fusion.5 = bf16[8,1024,1024]{1,2,0:T(8,128)(2,1)} fusion(f32[8,1024,1024]{1,2,0:T(8,128)} %get-tuple-element.442, f32[8,1024,1024]{1,2,0:T(8,128)} %fusion.144, f32[8,1024]{1,0:T(8,128)S(1)} %get-tuple-element.443, f32[8,1024]{1,0:T(8,128)S(1)} %dynamic-slice_bitcast_fusion.3), kind=kLoop, calls=%fused_computation.18.clone.1.clone | loop fusion | flops 41943040 | bytes 83951616 | tf_op jit(solution)/shard_map/while/body/eval_jaxpr/convert_element_type | solution.py:99
  1424.7 62.2 %all-reduce.18 = (bf16[3,640]{1,0:T(4,128)(2,1)S(1)}, bf16[2560]{0:T(1024)(128)(2,1)S(1)}) all-reduce(bf16[3,640]{1,0:T(4,128)(2,1)S(1)} %fusion.85, bf16[2560]{0:T(1024)(128)(2,1)S(1)} %copy-done.41), channel_id=9, replica_groups=mesh['dp'=16,'tensor'=2] {'dp'}, use_global_device_ids=true, to_apply=%region_25.26.clone | all-reduce | flops 4480 | bytes 17920
  1488.2 44.8 %all-reduce.21.cloned.1.call-done = bf16[3,1280,640]{2,0,1:T(4,128)(2,1)} async-done(((bf16[3,1280,640]{2,0,1:T(4,128)(2,1)}), bf16[3,1280,640]{2,0,1:T(4,128)(2,1)}) %all-reduce.21.cloned.1.call-update) | async-done | bytes 4915216
  1535.0 59.9 %reduce-scatter.17.cloned.1.call-done = bf16[640,80]{0,1:T(8,128)(2,1)} async-done(((bf16[640,1280]{0,1:T(8,128)(2,1)}), bf16[640,80]{0,1:T(8,128)(2,1)}) %reduce-scatter.17.cloned.1.call-update) | async-done | bytes 102416 | tf_op jit(solution)/shard_map/reduce_scatter | solution.py:282
  1596.5 65.4 %reduce-scatter.15.cloned.1.call-done = bf16[1024,1280]{1,0:T(8,128)(2,1)} async-done(((bf16[2048,1280]{1,0:T(8,128)(2,1)}), bf16[1024,1280]{1,0:T(8,128)(2,1)}) %reduce-scatter.15.cloned.1.call-update) | async-done | bytes 2621456 | tf_op jit(solution)/shard_map/reduce_scatter | solution.py:267
  1666.0 40.1 %all-reduce.16 = (f32[1280]{0:T(1024)S(1)}, f32[1280]{0:T(1024)S(1)}, f32[1280]{0:T(1024)S(1)}, f32[1280]{0:T(1024)S(1)}, f32[1280]{0:T(1024)S(1)}, /*index=5*/f32[1280]{0:T(1024)S(1)}) all-reduce(f32[1280]{0:T(1024)S(1)} %get-tuple-element.219, ...), channel_id=6, replica_groups=mesh['dp'=16,'tensor'=2] {'dp','tensor'}, use_global_device_ids=true, to_apply=%region_20.21.clone | all-reduce | flops 7680 | bytes 61440
  (339 shorter events, 801.7 us)
Async XLA Ops:
  7.3 120.9 %all-gather.10.cloned.1.call-start = ((), (), s32[]{:S(2)}) async-start(), calls=%async_computation.7 | async-start | bytes 7864320 | tf_op jit(solution)/shard_map/all_gather | solution.py:157
  59.5 125.0 %all-gather.12.cloned.1.call-start = ((), (), s32[]{:S(2)}) async-start(), calls=%async_computation.8 | async-start | bytes 5222400 | tf_op jit(solution)/shard_map/all_gather | solution.py:147
  60.3 329.3 %all-gather.14.cloned.1.call-start = ((), (), s32[]{:S(2)}) async-start(), calls=%async_computation.9 | async-start | bytes 1740800 | tf_op jit(solution)/shard_map/all_gather | solution.py:148
  61.0 401.8 %reduce-scatter.9.cloned.1.call-start = ((), (), s32[]{:S(2)}) async-start(), calls=%async_computation.10 | async-start | bytes 7864320 | tf_op jit(solution)/shard_map/reduce_scatter | solution.py:178
  398.5 211.8 %all-gather.18.cloned.1.call-start = ((), (), s32[]{:S(2)}) async-start(), calls=%async_computation.12 | async-start | bytes 6963200 | tf_op jit(solution)/shard_map/all_gather | solution.py:149
  399.1 229.9 %all-gather.16.cloned.1.call-start = ((), (), s32[]{:S(2)}) async-start(), calls=%async_computation.11 | async-start | bytes 7864320 | tf_op jit(solution)/shard_map/all_gather | solution.py:187
  470.4 228.7 %all-gather.20.cloned.1.call-start = ((), (), s32[]{:S(2)}) async-start(), calls=%async_computation.14 | async-start | bytes 7864320 | tf_op jit(solution)/shard_map/all_gather | solution.py:209
  471.1 293.1 %all-gather.22.cloned.1.call-start = ((), (), s32[]{:S(2)}) async-start(), calls=%async_computation.15 | async-start | bytes 6963200 | tf_op jit(solution)/shard_map/all_gather | solution.py:205
  471.9 406.3 %reduce-scatter.13.cloned.1.call-start = ((), (), s32[]{:S(2)}) async-start(), calls=%async_computation.16 | async-start | bytes 7864320 | tf_op jit(solution)/shard_map/reduce_scatter | solution.py:221
  471.9 16.8 collective-permute-start
  499.6 16.4 collective-permute-start.2
  499.6 19.0 %collective-permute-start.9 = (bf16[2560,80]{0,1:T(8,128)(2,1)S(1)}, bf16[2560,80]{0,1:T(8,128)(2,1)S(1)}, u32[]{:S(2)}, u32[]{:S(2)}) collective-permute-start(bf16[2560,80]{0,1:T(8,128)(2,1)S(1)} %collective-permute-done.8), channel_id=1, source_target_pairs={{2,0},{4,2},{6,4},{8,6},{10,8},{12,10},{14,12},{16,14},{18,16},{20... | collective-permute-start | bytes 1228808 | tf_op jit(solution)/shard_map/ppermute | solution.py:28
  529.5 14.1 collective-permute-start.4
  529.5 17.7 %collective-permute-start.11 = (bf16[2560,80]{0,1:T(8,128)(2,1)S(1)}, bf16[2560,80]{0,1:T(8,128)(2,1)S(1)}, u32[]{:S(2)}, u32[]{:S(2)}) collective-permute-start(bf16[2560,80]{0,1:T(8,128)(2,1)S(1)} %collective-permute-done.10), channel_id=1, source_target_pairs={{2,0},{4,2},{6,4},{8,6},{10,8},{12,10},{14,12},{16,14},{18,16},{20... | collective-permute-start | bytes 1228808 | tf_op jit(solution)/shard_map/ppermute | solution.py:28
  557.3 44.1 %collective-permute-start.13 = (bf16[2560,80]{0,1:T(8,128)(2,1)}, bf16[2560,80]{0,1:T(8,128)(2,1)}, u32[]{:S(2)}, u32[]{:S(2)}) collective-permute-start(bf16[2560,80]{0,1:T(8,128)(2,1)} %collective-permute-done.12), channel_id=1, source_target_pairs={{2,0},{4,2},{6,4},{8,6},{10,8},{12,10},{14,12},{16,14},{18,16},{20... | collective-permute-start | bytes 1228808 | tf_op jit(solution)/shard_map/ppermute | solution.py:28
  565.4 36.1 %collective-permute-start.7 = (bf16[2560,80]{0,1:T(8,128)(2,1)}, bf16[2560,80]{0,1:T(8,128)(2,1)}, u32[]{:S(2)}, u32[]{:S(2)}) collective-permute-start(bf16[2560,80]{0,1:T(8,128)(2,1)} %collective-permute-done.6), channel_id=1, source_target_pairs={{0,2},{2,4},{4,6},{6,8},{8,10},{10,12},{12,14},{14,16},{16,18},{18... | collective-permute-start | bytes 1228808 | tf_op jit(solution)/shard_map/ppermute | solution.py:26
  601.4 222.4 %collective-permute-start.14 = (bf16[2560,80]{0,1:T(8,128)(2,1)}, bf16[2560,80]{0,1:T(8,128)(2,1)}, u32[]{:S(2)}, u32[]{:S(2)}) collective-permute-start(bf16[2560,80]{0,1:T(8,128)(2,1)} %collective-permute-done.13), channel_id=1, source_target_pairs={{2,0},{4,2},{6,4},{8,6},{10,8},{12,10},{14,12},{16,14},{18,16},{20... | collective-permute-start | bytes 1228808 | tf_op jit(solution)/shard_map/ppermute | solution.py:28
  813.5 132.6 %reduce-scatter.11.cloned.1.call-start = ((), (), s32[]{:S(2)}) async-start(), calls=%async_computation.13 | async-start | bytes 7864320 | tf_op jit(solution)/shard_map/reduce_scatter | solution.py:194
  851.6 172.6 %all-gather.24.cloned.1.call-start = ((), (), s32[]{:S(2)}) async-start(), calls=%async_computation.17 | async-start | bytes 7864320 | tf_op jit(solution)/shard_map/all_gather | solution.py:234
  955.5 460.3 %reduce-scatter.21.cloned.1.call-start = ((), (), s32[]{:S(2)}) async-start(), calls=%async_computation.21 | async-start | bytes 6963200 | tf_op jit(solution)/shard_map/reduce_scatter | solution.py:288
  976.0 441.7 %reduce-scatter.19.cloned.1.call-start = ((), (), s32[]{:S(2)}) async-start(), calls=%async_computation.20 | async-start | bytes 6963200 | tf_op jit(solution)/shard_map/reduce_scatter | solution.py:285
  1008.8 524.3 %all-reduce.21.cloned.1.call-start = ((), (), s32[]{:S(2)}) async-start(), calls=%async_computation.22 | async-start | bytes 13107200
  1388.7 206.2 %reduce-scatter.17.cloned.1.call-start = ((), (), s32[]{:S(2)}) async-start(), calls=%async_computation.19 | async-start | bytes 1740800 | tf_op jit(solution)/shard_map/reduce_scatter | solution.py:282
  1397.6 264.3 %reduce-scatter.15.cloned.1.call-start = ((), (), s32[]{:S(2)}) async-start(), calls=%async_computation.18 | async-start | bytes 7864320 | tf_op jit(solution)/shard_map/reduce_scatter | solution.py:267
  (66 other events, 3125.0 us)
Sparse Core Ops, SparseCore 0:
  59.6 68.4 all-gather.9
  130.4 54.1 all-gather.11
  186.7 38.4 all-gather.13
  398.6 64.1 reduce-scatter.8
  464.9 85.3 all-gather.17
  552.2 76.6 all-gather.15
  630.5 68.5 all-gather.19
  701.4 62.8 all-gather.21
  813.6 64.4 reduce-scatter.12
  880.3 65.7 reduce-scatter.10
  955.6 68.5 all-gather.23
  1028.0 86.7 reduce-scatter.20
  1118.8 85.7 reduce-scatter.18
  1388.9 144.1 all-reduce.20
  1536.7 58.1 reduce-scatter.16
  1597.0 64.7 reduce-scatter.14
